TPU v7x, 256 devices: a whole 4x4x8 slice. The times are simulated.
256 devices in a mesh: box: 2 (over x_hi), dir: 128 (over z, y, x_lo, core).
Axes of the slice: x: 4 (x_hi: 2, x_lo: 2; x = x_hi * 2 + x_lo), y: 4, z: 8, core: 2. Of those that a mesh axis runs over, the one named last changes fastest.
Arguments:
- leaf_patterns: bfloat16 [4096, 2, 8, 1024], P(('box', 'dir')), may hold values from -6 to 6
- octant: int32 [4096], P(('box', 'dir')), may hold values from 0 to 7, as said below
- interp: bfloat16 [1024, 4096], replicated, may hold values from -0.1875 to 0.1875
- shift_angle: float32 [8, 4096], replicated, may hold values from -3.140625 to 3.140625
- partners: int32 [512, 27], P('box'), may hold values from 0 to 511, as said below
- types: int32 [512, 27], P('box'), may hold values from 0 to 342, as said below
- translators: float32 [343, 2, 4096], P(None, None, 'dir'), may hold values from -1 to 1
Outputs:
- leaf_incoming: bfloat16 [4096, 2, 8, 1024], P(('box', 'dir'))
Inputs may be any that keep to these rules, and one draw needn't show every extreme that they name: The leaf boxes 8 p to 8 p + 7 are the children of parent box p; octant gives each child its position in the parent, each of 0 to 7 once among the 8 children. Parent boxes form a grid indexed in Morton order (bit j of the index is a bit of coordinate j % 3). The 27 partners of a box are distinct boxes within three boxes of it along every dimension, and none is the box itself or one of its 26 neighbours. types[p, k] = 49 (dx + 3) + 7 (dy + 3) + (dz + 3), where (dx, dy, dz) is the grid offset from box p to partners[p, k].
All inputs are finite; a program needn't handle non-finite values.
Results may differ from a plain program's by a relative error of at most 0.0064.
Values may be sent and summed in bfloat16 or wider, within the bound.
A program may use at most 64 MiB of HBM per device.

v0:
```python
import jax
import jax.numpy as jnp
from jax import lax
from jax.sharding import PartitionSpec as P


def local(leaf_patterns, octant, interp, shift_angle, partners, types, translators):
    boxes, pairs, excite, low = leaf_patterns.shape
    high = interp.shape[1]
    groups = lax.axis_size("dir")
    width = high // groups
    parents = boxes // 8
    columns = 2 * excite * width
    cosines = jnp.cos(shift_angle)
    sines = jnp.sin(shift_angle)
    select = (octant[:, None] == jnp.arange(8, dtype=jnp.int32)[None, :]).astype(jnp.float32)
    child_cos = jnp.dot(select, cosines, precision=lax.Precision.HIGHEST)[:, None, :]
    child_sin = jnp.dot(select, sines, precision=lax.Precision.HIGHEST)[:, None, :]
    up = jnp.dot(leaf_patterns.reshape(-1, low), interp, preferred_element_type=jnp.float32)
    up = up.reshape(boxes, 2, excite, high)
    real = up[:, 0] * child_cos - up[:, 1] * child_sin
    imag = up[:, 0] * child_sin + up[:, 1] * child_cos
    aggregated = (
        jnp.stack([real, imag], 1)
        .reshape(parents, 8, 2, excite, high)
        .sum(axis=1)
        .astype(jnp.bfloat16)
    )
    outgoing = aggregated.reshape(parents, 2, excite, groups, width).transpose(0, 3, 1, 2, 4)
    outgoing = outgoing.reshape(parents, groups, columns)
    regrouped = lax.all_to_all(outgoing, "dir", split_axis=1, concat_axis=0, tiled=True).reshape(
        parents * groups, columns
    )
    every = lax.all_gather(regrouped, "box", axis=0, tiled=True)
    owned = partners.shape[0]
    linked = partners.shape[1]

    def translate(step, total):
        source = (
            jnp.take(every, partners[:, step], axis=0)
            .reshape(owned, 2, excite, width)
            .astype(jnp.float32)
        )
        factor = jnp.take(translators, types[:, step], axis=0)
        factor_re = factor[:, 0][:, None, :]
        factor_im = factor[:, 1][:, None, :]
        real_part = factor_re * source[:, 0] - factor_im * source[:, 1]
        imag_part = factor_re * source[:, 1] + factor_im * source[:, 0]
        return total + jnp.stack([real_part, imag_part], 1)

    zero = jnp.zeros((owned, 2, excite, width), jnp.float32)
    summed = lax.fori_loop(0, linked, translate, zero)
    incoming = summed.astype(jnp.bfloat16).reshape(groups, parents, 1, columns)
    returned = lax.all_to_all(incoming, "dir", split_axis=0, concat_axis=2, tiled=True)
    returned = returned.reshape(parents, groups, 2, excite, width).transpose(0, 2, 3, 1, 4)
    returned = returned.reshape(parents, 1, 2, excite, high).astype(jnp.float32)
    spread_cos = child_cos.reshape(parents, 8, 1, 1, high)
    spread_sin = child_sin.reshape(parents, 8, 1, 1, high)
    real = returned[:, :, 0] * spread_cos[:, :, 0] + returned[:, :, 1] * spread_sin[:, :, 0]
    imag = returned[:, :, 1] * spread_cos[:, :, 0] - returned[:, :, 0] * spread_sin[:, :, 0]
    shifted = jnp.stack([real, imag], 2).astype(jnp.bfloat16).reshape(-1, high)
    down = lax.dot_general(
        shifted, interp, (((1,), (1,)), ((), ())), preferred_element_type=jnp.float32
    )
    scale = low / high
    return (down * scale).astype(jnp.bfloat16).reshape(boxes, 2, excite, low)


def solution(mesh):
    placed = (
        P(("box", "dir"), None, None, None),
        P(("box", "dir")),
        P(),
        P(),
        P("box", None),
        P("box", None),
        P(None, None, "dir"),
    )
    return jax.shard_map(
        local,
        mesh=mesh,
        in_specs=placed,
        out_specs=P(("box", "dir"), None, None, None),
        check_vma=False,
    )
```

profile of v0, /device:TPU:1, one launch (start us, length us, event | category | flops | bytes accessed | tf_op | source)
XLA Modules:
  0.0 194.7 jit_solution(3032233438941313428)
XLA Ops:
  0.0 1.6 fusion.3
  1.6 1.6 fusion.5
  3.2 5.7 %fusion = f32[16,2,8,4096]{3,2,1,0:T(8,128)S(1)} fusion(bf16[16,2,8,1024]{3,2,1,0:T(8,128)(2,1)S(1)} %copy-done, bf16[1024,4096]{1,0:T(8,128)(2,1)} %param.11), kind=kOutput, calls=%fused_computation.13 | convolution fusion | flops 2147483648 | bytes 13107200 | tf_op jit(solution)/shard_map/dot_general | solution.py:19
  12.0 14.9 %all-to-all-start = ((bf16[2,128,512]{2,0,1:T(2,128)(2,1)}), bf16[2,128,512]{2,0,1:T(2,128)(2,1)S(1)}, u32[]{:S(2)}, u32[]{:S(2)}) async-start(bf16[2,128,512]{2,0,1:T(2,128)(2,1)} %copy.32), calls=%async_computation | async-start | bytes 524288 | tf_op jit(solution)/shard_map/all_to_all | solution.py:31
  27.1 13.3 %all-to-all-done = bf16[2,128,512]{2,0,1:T(2,128)(2,1)S(1)} async-done(((bf16[2,128,512]{2,0,1:T(2,128)(2,1)}), bf16[2,128,512]{2,0,1:T(2,128)(2,1)S(1)}, u32[]{:S(2)}, u32[]{:S(2)}) %all-to-all-start) | async-done | bytes 262176 | tf_op jit(solution)/shard_map/all_to_all | solution.py:31
  40.5 8.1 %all_gather.3 = bf16[512,512]{1,0:T(8,128)(2,1)S(1)} all-gather(bf16[256,512]{1,0:T(8,128)(2,1)S(1)} %reshape.94), channel_id=1, replica_groups=mesh['box'=2,'dir'=128] {'box'}, dimensions={0}, use_global_device_ids=true | all-gather | bytes 786432 | tf_op jit(solution)/shard_map/all_gather | solution.py:34
  48.6 109.8 %while.14 = (s32[]{:T(128)}, f32[256,2,8,32]{0,3,2,1:T(8,128)S(1)}, s32[256,27]{0,1:T(8,128)}, f32[343,2,32]{2,1,0:T(2,128)S(1)}, s32[256,27]{0,1:T(8,128)}, /*i...) while((s32[]{:T(128)}, f32[256,2,8,32]{0,3,2,1:T(8,128)S(1)}, s32[256,27]{0,1:T(8,128)}, ...), condition=%wide.region_2.0_spmd.clone, body=%wide.region_1.2_spmd.clone.sunk | while | flops 1070083 | bytes 5063779 | solution.py:52
  49.4 1.0 gather_fusion.1
  51.1 1.2 gather_fusion
  53.5 1.0 gather_fusion.1
  55.2 1.2 gather_fusion
  57.5 1.0 gather_fusion.1
  59.2 1.2 gather_fusion
  61.6 1.0 gather_fusion.1
  63.3 1.2 gather_fusion
  65.7 1.0 gather_fusion.1
  67.4 1.2 gather_fusion
  69.7 1.0 gather_fusion.1
  71.4 1.2 gather_fusion
  73.8 1.0 gather_fusion.1
  75.5 1.2 gather_fusion
  77.9 1.0 gather_fusion.1
  79.6 1.2 gather_fusion
  81.9 1.0 gather_fusion.1
  83.6 1.2 gather_fusion
  86.0 1.0 gather_fusion.1
  87.7 1.2 gather_fusion
  91.8 1.2 gather_fusion
  94.1 1.0 gather_fusion.1
  95.8 1.2 gather_fusion
  98.2 1.0 gather_fusion.1
  99.9 1.2 gather_fusion
  102.3 1.0 gather_fusion.1
  104.0 1.2 gather_fusion
  106.4 1.0 gather_fusion.1
  108.1 1.2 gather_fusion
  110.4 1.0 gather_fusion.1
  112.1 1.2 gather_fusion
  114.5 1.0 gather_fusion.1
  116.2 1.2 gather_fusion
  118.6 1.0 gather_fusion.1
  120.3 1.2 gather_fusion
  122.6 1.0 gather_fusion.1
  124.3 1.2 gather_fusion
  126.7 1.0 gather_fusion.1
  128.4 1.2 gather_fusion
  132.5 1.2 gather_fusion
  134.8 1.0 gather_fusion.1
  136.5 1.2 gather_fusion
  138.9 1.0 gather_fusion.1
  140.6 1.2 gather_fusion
  143.0 1.0 gather_fusion.1
  144.7 1.2 gather_fusion
  147.0 1.0 gather_fusion.1
  148.7 1.2 gather_fusion
  151.1 1.0 gather_fusion.1
  152.8 1.2 gather_fusion
  155.2 1.0 gather_fusion.1
  156.9 1.2 gather_fusion
  160.3 21.6 %all_to_all.27 = bf16[128,2,1,512]{3,1,2,0:T(2,128)(2,1)S(1)} all-to-all(bf16[128,2,1,512]{3,1,2,0:T(2,128)(2,1)S(1)} %bitcast.66), channel_id=1, replica_groups=mesh['box'=2,'dir'=128] {'dir'}, dimensions={0} | all-to-all | bytes 524288 | tf_op jit(solution)/shard_map/all_to_all | solution.py:54
  183.0 1.6 copy.37
  184.7 1.7 reshape.97
  186.4 1.1 slice_bitcast_fusion.1
  188.2 6.5 %fusion.2 = bf16[256,1024]{1,0:T(8,128)(2,1)} fusion(bf16[256,4096]{1,0:T(8,128)(2,1)S(1)} %bitcast.64, bf16[1024,4096]{1,0:T(8,128)(2,1)} %param.11), kind=kOutput, calls=%fused_computation.22 | convolution fusion | flops 2148007936 | bytes 11010048 | tf_op jit(solution)/shard_map/dot_general | solution.py:62
  (319 shorter events, 58.9 us)
Async XLA Ops:
  0.0 3.2 %copy-start = (bf16[16,2,8,1024]{3,2,1,0:T(8,128)(2,1)S(1)}, bf16[16,2,8,1024]{3,2,1,0:T(8,128)(2,1)}, u32[]{:S(2)}) copy-start(bf16[16,2,8,1024]{3,2,1,0:T(8,128)(2,1)} %param.9) | copy-start | bytes 1572868
  9.9 17.0 %copy-start.1 = (f32[343,2,32]{0,2,1:T(8,128)S(1)}, f32[343,2,32]{0,2,1:T(8,128)}, u32[]{:S(2)}) copy-start(f32[343,2,32]{0,2,1:T(8,128)} %param.15) | copy-start | bytes 263428
  12.0 28.4 %all-to-all-start = ((bf16[2,128,512]{2,0,1:T(2,128)(2,1)}), bf16[2,128,512]{2,0,1:T(2,128)(2,1)S(1)}, u32[]{:S(2)}, u32[]{:S(2)}) async-start(bf16[2,128,512]{2,0,1:T(2,128)(2,1)} %copy.32), calls=%async_computation | async-start | bytes 524288 | tf_op jit(solution)/shard_map/all_to_all | solution.py:31
where the time goes:
time: 198 us; the launch traced here: 195 us
  local copies, waits for them, and re-layouts  79.1 us (40%)
  other arithmetic  39.8 us (20%)
  blocking collectives  29.8 us (15%)
  matrix products  15.5 us (8%)
  starting transfers between devices  14.9 us (8%)
  waiting for transfers between devices  13.3 us (7%)
  loops' own time  2.23 us (1%)
    gather x54, local copies, waits for them, and re-layouts, translate(): jnp.take(every, partners[:, step], axis=0).reshape(owned, 2, excite, width)  34.7 us
    gather x27, local copies, waits for them, and re-layouts, translate(): factor = jnp.take(translators, types[:, step], axis=0)  26.4 us
    all_to_all x1, blocking collectives, local(): lax.all_to_all(incoming, 'dir', split_axis=0, concat_axis=2, tiled=True)  21.6 us
    and x27, other arithmetic, translate(): jnp.take(every, partners[:, step], axis=0).reshape(owned, 2, excite, width)  20.1 us
    all_to_all x1, starting transfers between devices, local(): lax.all_to_all(outgoing, 'dir', split_axis=1, concat_axis=0, tiled=True)  14.9 us
    all_to_all x1, waiting for transfers between devices, local(): lax.all_to_all(outgoing, 'dir', split_axis=1, concat_axis=0, tiled=True)  13.3 us
    select_n x27, other arithmetic, translate(): factor = jnp.take(translators, types[:, step], axis=0)  9.07 us
    all_gather x1, blocking collectives, local(): every = lax.all_gather(regrouped, 'box', axis=0, tiled=True)  8.12 us
  transfers between devices with their start and end apart: 1, of which 1 were waited for; matrix products, arithmetic and copies ran while one was open for 0% of the time, Pallas kernels for 0%

commit v1 on v0

v1 whole, which is shorter than its diff:
```python
import jax
import jax.numpy as jnp
from jax import lax
from jax.experimental import pallas as pl
from jax.experimental.pallas import tpu as pltpu
from jax.sharding import PartitionSpec as P

MESH = pl.DeviceIdType.MESH
Z = 8
PLANE = 32
WIDTH = 16
CHUNK = PLANE * WIDTH
PB = 64
LINKED = 27
ROWS = PB * LINKED
BLOCKS = Z * 2 * PLANE // PB
TYPES = 384
F32, BF16 = jnp.float32, jnp.bfloat16


def block_transpose(xs):
    block = lax.broadcasted_iota(jnp.int32, xs[0].shape, 1) // 16
    for step in (1, 2, 4):
        low = (block // step) % 2 == 0
        out = list(xs)
        for i in range(8):
            if i & step == 0:
                a, b = xs[i], xs[i + step]
                out[i] = jnp.where(low, a, pltpu.roll(b, 16 * step, 1))
                out[i + step] = jnp.where(low, pltpu.roll(a, 128 - 16 * step, 1), b)
        xs = out
    return xs


def kernel(
    oct_ref, leaf_ref, interp_ref, cos_ref, sin_ref, idx_ref, tr_ref, out_ref,
    interp_v, zsend, zrecv, ysend, arecv, idxall, oht, oh, fac, rsend, rrecv, xp, wsend, wrecv, shifted, acc,
    isem, zs, zr, ys, yr, xs_sem, xr_sem, rs, rr, ws, wr,
):
    box = lax.axis_index("box")
    d = lax.axis_index("dir")
    z = d // 16
    yxc = d % 16
    slab = box * 16 + yxc
    spot = yxc * 2 + box

    def plane_of_slab(s):
        return (s // 16, z * 16 + s % 16)

    def plane_of_spot(t):
        return (t % 2, z * 16 + t // 2)

    def order(i):
        half = (i + 1) // 2
        return (z + 4 + half * (1 - 2 * (i % 2))) % 8

    def fetch(i):
        zc = order(i)
        at = pl.multiple_of(zc * CHUNK, CHUNK)
        return pltpu.make_async_copy(interp_ref.at[:, pl.ds(at, CHUNK)], interp_v.at[zc], isem.at[i])

    for i in range(Z):
        fetch(i).start()

    barrier = pltpu.get_barrier_semaphore()

    def greet_z(i, carry):
        pl.semaphore_signal(barrier, inc=1, device_id=(box, (z + i) % 8 * 16 + yxc), device_id_type=MESH)
        return carry

    def greet_plane(i, carry):
        pl.semaphore_signal(barrier, inc=1, device_id=plane_of_slab((slab + i) % PLANE), device_id_type=MESH)
        return carry

    lax.fori_loop(1, Z, greet_z, 0)
    lax.fori_loop(1, PLANE, greet_plane, 0)
    pl.semaphore_wait(barrier, Z - 1 + PLANE - 1)

    idx_copy = pltpu.make_async_remote_copy(
        src_ref=idx_ref, dst_ref=idxall.at[box], send_sem=xs_sem, recv_sem=xr_sem,
        device_id=(1 - box, d), device_id_type=MESH,
    )
    idx_copy.start()

    def z_copy(src, dst, ssem, rsem, zc):
        return pltpu.make_async_remote_copy(
            src_ref=src.at[zc], dst_ref=dst.at[z], send_sem=ssem.at[zc], recv_sem=rsem.at[z],
            device_id=(box, zc * 16 + yxc), device_id_type=MESH,
        )

    def z_arrival(src, dst, ssem, rsem, zc):
        return pltpu.make_async_remote_copy(
            src_ref=src.at[zc], dst_ref=dst.at[zc], send_sem=ssem.at[zc], recv_sem=rsem.at[zc],
            device_id=(box, zc * 16 + yxc), device_id_type=MESH,
        )

    def phases(child, zc):
        o = oct_ref[child]
        at = pl.ds(pl.multiple_of(zc * CHUNK, CHUNK), CHUNK)
        return cos_ref[pl.ds(o, 1), at], sin_ref[pl.ds(o, 1), at]

    def lift(i, carry):
        zc = order(i)
        fetch(i).wait()
        up = jnp.dot(leaf_ref[...], interp_v[zc], preferred_element_type=F32)
        parts = []
        for parent in range(2):
            real = imag = None
            for k in range(8):
                child = parent * 8 + k
                cs, sn = phases(child, zc)
                ur, ui = up[child * 16 : child * 16 + 8], up[child * 16 + 8 : child * 16 + 16]
                a, b = ur * cs - ui * sn, ur * sn + ui * cs
                real, imag = (a, b) if real is None else (real + a, imag + b)
            parts += [real, imag]
        zsend[zc] = jnp.concatenate(parts, axis=0).astype(BF16)

        @pl.when(i < Z - 1)
        def _():
            z_copy(zsend, zrecv, zs, zr, zc).start()

        return carry

    lax.fori_loop(0, Z, lift, 0)
    zrecv[z] = zsend[z]

    idxall[box] = idx_ref[...]
    spread = (
        lax.broadcasted_iota(jnp.int32, (64, 256), 0)
        == lax.broadcasted_iota(jnp.int32, (64, 256), 1) // 128 * 32
        + box * WIDTH
        + lax.broadcasted_iota(jnp.int32, (64, 256), 1) % WIDTH
    )
    table = jnp.dot(tr_ref[...], spread.astype(F32).astype(BF16), preferred_element_type=F32).astype(BF16)
    idx_copy.wait()

    def indices(pb):
        half = BLOCKS // 2
        return idxall[pb // half, pl.ds(pl.multiple_of(pb % half * PB, PB), PB), :]

    def factors(pb, carry):
        index = indices(pb)
        wide = lax.broadcasted_iota(jnp.int32, (PB, TYPES), 1)
        for k in range(LINKED):
            oht[k * PB : (k + 1) * PB, :] = (wide == index[:, 32 + k : 33 + k]).astype(F32).astype(BF16)
        fac[pb] = jnp.dot(oht[...], table, preferred_element_type=F32)
        return carry

    lax.fori_loop(0, BLOCKS, factors, 0)

    def z_wait(i, carry):
        zc = (z + i) % 8
        z_arrival(zsend, zrecv, zs, zr, zc).wait_recv()
        return carry

    lax.fori_loop(1, Z, z_wait, 0)

    r0 = lax.broadcasted_iota(jnp.int32, (256, 256), 0)
    r1 = lax.broadcasted_iota(jnp.int32, (256, 256), 1)
    turn = (r1 == r0 % 16 * 16 + r0 // 16).astype(F32).astype(BF16)
    turned = jnp.dot(turn, zrecv[...].reshape(256, CHUNK), preferred_element_type=F32)
    for pair in range(2):
        for dh in range(4):
            lanes = slice(dh * 128, dh * 128 + 128)
            blocks = [turned[(pair * 8 + j) * 16 : (pair * 8 + j) * 16 + 16, lanes] for j in range(8)]
            for j, y in enumerate(block_transpose(blocks)):
                ysend[dh * 8 + j, :, pair * 128 : pair * 128 + 128] = y.astype(BF16)

    def y_copy(t):
        return pltpu.make_async_remote_copy(
            src_ref=ysend.at[t], dst_ref=arecv.at[slab], send_sem=ys.at[t], recv_sem=yr.at[slab],
            device_id=plane_of_spot(t), device_id_type=MESH,
        )

    def y_arrival(s):
        return pltpu.make_async_remote_copy(
            src_ref=ysend.at[s], dst_ref=arecv.at[s], send_sem=ys.at[s], recv_sem=yr.at[s],
            device_id=plane_of_slab(s), device_id_type=MESH,
        )

    def y_start(i, carry):
        y_copy((spot + i) % PLANE).start()
        return carry

    lax.fori_loop(1, PLANE, y_start, 0)
    arecv[slab] = ysend[spot]

    def sources(pb, carry):
        index = indices(pb)
        wide = lax.broadcasted_iota(jnp.int32, (PB, 512), 1)
        for k in range(LINKED):
            oh[pb, k * PB : (k + 1) * PB, :] = (wide == index[:, k : k + 1]).astype(F32).astype(BF16)
        return carry

    lax.fori_loop(0, BLOCKS, sources, 0)

    def y_wait(i, carry):
        y_arrival((slab + i) % PLANE).wait_recv()
        return carry

    lax.fori_loop(1, PLANE, y_wait, 0)

    def r_copy(s):
        return pltpu.make_async_remote_copy(
            src_ref=rsend.at[s], dst_ref=rrecv.at[spot], send_sem=rs.at[s], recv_sem=rr.at[spot],
            device_id=plane_of_slab(s), device_id_type=MESH,
        )

    def r_arrival(t):
        return pltpu.make_async_remote_copy(
            src_ref=rsend.at[t], dst_ref=rrecv.at[t], send_sem=rs.at[t], recv_sem=rr.at[t],
            device_id=plane_of_spot(t), device_id_type=MESH,
        )

    def translate(pb, carry):
        got = jnp.dot(oh[pb], arecv[...].reshape(512, 256), preferred_element_type=F32)
        real = imag = None
        for k in range(LINKED):
            rows = slice(k * PB, (k + 1) * PB)
            fr, fi = fac[pb, rows, 0:128], fac[pb, rows, 128:256]
            sr, si = got[rows, 0:128], got[rows, 128:256]
            a, b = fr * sr - fi * si, fr * si + fi * sr
            real, imag = (a, b) if real is None else (real + a, imag + b)
        each = jnp.concatenate([real, imag], axis=1).astype(BF16)
        for j in range(PB // 16):
            s = pb * (PB // 16) + j
            rsend[s] = each[j * 16 : j * 16 + 16]

            @pl.when(s != slab)
            def _():
                r_copy(s).start()

        return carry

    lax.fori_loop(0, BLOCKS, translate, 0)
    rrecv[spot] = rsend[slab]

    def r_wait(i, carry):
        r_arrival((spot + i) % PLANE).wait_recv()
        return carry

    lax.fori_loop(1, PLANE, r_wait, 0)

    for pair in range(2):
        for dh in range(4):
            lanes = slice(dh * 128, dh * 128 + 128)
            blocks = [rrecv[dh * 8 + j, :, pair * 128 : pair * 128 + 128].astype(F32) for j in range(8)]
            for j, y in enumerate(block_transpose(blocks)):
                xp[(pair * 8 + j) * 16 : (pair * 8 + j) * 16 + 16, lanes] = y.astype(BF16)
    wsend[...] = jnp.dot(turn, xp[...], preferred_element_type=F32).astype(BF16).reshape(Z, 32, CHUNK)

    def w_start(i, carry):
        z_copy(wsend, wrecv, ws, wr, order(i)).start()
        return carry

    lax.fori_loop(0, Z - 1, w_start, 0)
    wrecv[z] = wsend[z]
    acc[...] = jnp.zeros_like(acc)

    def descend(i, carry):
        zc = order(Z - 1 - i)

        @pl.when(i > 0)
        def _():
            z_arrival(wsend, wrecv, ws, wr, zc).wait_recv()

        got = wrecv[zc].astype(F32)
        for parent in range(2):
            re, im = got[parent * 16 : parent * 16 + 8], got[parent * 16 + 8 : parent * 16 + 16]
            for k in range(8):
                child = parent * 8 + k
                cs, sn = phases(child, zc)
                both = jnp.concatenate([re * cs + im * sn, im * cs - re * sn], axis=0)
                shifted[child * 16 : child * 16 + 16, :] = both.astype(BF16)
        acc[...] += lax.dot_general(
            shifted[...], interp_v[zc], (((1,), (1,)), ((), ())), preferred_element_type=F32
        )
        return carry

    lax.fori_loop(0, Z, descend, 0)
    out_ref[...] = (acc[...] * 0.25).astype(BF16)

    def z_sent(i, carry):
        zc = (z + i) % 8
        z_copy(zsend, zrecv, zs, zr, zc).wait_send()
        z_copy(wsend, wrecv, ws, wr, zc).wait_send()
        return carry

    def plane_sent(i, carry):
        y_copy((spot + i) % PLANE).wait_send()
        r_copy((slab + i) % PLANE).wait_send()
        return carry

    lax.fori_loop(1, Z, z_sent, 0)
    lax.fori_loop(1, PLANE, plane_sent, 0)


def local(leaf_patterns, octant, interp, shift_angle, partners, types, translators):
    boxes, pairs, excite, low = leaf_patterns.shape
    high = interp.shape[1]
    own = partners.shape[0]
    place = (partners // 256 * 16 + partners // 2 % 16) * 16 + partners // 32 % 8 * 2 + partners % 2

    def lay(x):
        x = x.reshape(Z, own // Z // 2, 2, LINKED).transpose(1, 0, 2, 3).reshape(own, LINKED)
        return jnp.pad(x, ((0, 0), (0, 32 - LINKED)))

    index = jnp.pad(jnp.concatenate([lay(place), lay(types)], axis=1), ((0, 0), (0, 64)))
    offsets = translators.shape[0]
    tr = jnp.pad(translators.reshape(offsets, -1).astype(BF16), ((0, TYPES - offsets), (0, 0)))
    rows = boxes * pairs * excite
    vmem = pl.BlockSpec(memory_space=pltpu.VMEM)
    dma = pltpu.SemaphoreType.DMA
    out = pl.pallas_call(
        kernel,
        out_shape=jax.ShapeDtypeStruct((rows, low), BF16),
        in_specs=[
            pl.BlockSpec(memory_space=pltpu.SMEM),
            vmem,
            pl.BlockSpec(memory_space=pl.ANY),
            vmem,
            vmem,
            vmem,
            vmem,
        ],
        out_specs=vmem,
        scratch_shapes=[
            pltpu.VMEM((Z, low, CHUNK), BF16),
            pltpu.VMEM((Z, 32, CHUNK), BF16),
            pltpu.VMEM((Z, 32, CHUNK), BF16),
            pltpu.VMEM((PLANE, 16, 256), BF16),
            pltpu.VMEM((PLANE, 16, 256), BF16),
            pltpu.VMEM((2, own, 128), jnp.int32),
            pltpu.VMEM((ROWS, TYPES), BF16),
            pltpu.VMEM((BLOCKS, ROWS, 512), BF16),
            pltpu.VMEM((BLOCKS, ROWS, 256), F32),
            pltpu.VMEM((PLANE, 16, 256), BF16),
            pltpu.VMEM((PLANE, 16, 256), BF16),
            pltpu.VMEM((256, CHUNK), BF16),
            pltpu.VMEM((Z, 32, CHUNK), BF16),
            pltpu.VMEM((Z, 32, CHUNK), BF16),
            pltpu.VMEM((rows, CHUNK), BF16),
            pltpu.VMEM((rows, low), F32),
            dma((Z,)), dma((Z,)), dma((Z,)), dma((PLANE,)), dma((PLANE,)), dma, dma,
            dma((PLANE,)), dma((PLANE,)), dma((Z,)), dma((Z,)),
        ],
        compiler_params=pltpu.CompilerParams(
            collective_id=0, has_side_effects=True, vmem_limit_bytes=60 * 1024 * 1024
        ),
    )(
        octant,
        leaf_patterns.reshape(rows, low),
        interp,
        jnp.cos(shift_angle),
        jnp.sin(shift_angle),
        index,
        tr,
    )
    return out.reshape(boxes, pairs, excite, low)


def solution(mesh):
    placed = (
        P(("box", "dir"), None, None, None),
        P(("box", "dir")),
        P(),
        P(),
        P("box", None),
        P("box", None),
        P(None, None, "dir"),
    )
    return jax.shard_map(
        local,
        mesh=mesh,
        in_specs=placed,
        out_specs=P(("box", "dir"), None, None, None),
        check_vma=False,
    )
```

time: 198 us -> 60.7 us (0.31)
  the two profiles are of different devices: /device:TPU:1 before, /device:TPU:13 now
where the time goes in v1:
time: 60.7 us; the launch traced here: 60.4 us
  Pallas kernels  51.8 us (85%)
  local copies, waits for them, and re-layouts  7.23 us (12%)
  other arithmetic  1.34 us (2%)
    pallas_call x1, Pallas kernels, local(): pl.pallas_call(kernel, out_shape=jax.ShapeDtypeStruct((rows, low), BF16),...  51.8 us
    unnamed x3, local copies, waits for them, and re-layouts  3.61 us
    sin x1, local copies, waits for them, and re-layouts, local(): jnp.sin(shift_angle)  2.06 us

profile of v1, /device:TPU:13, one launch (start us, length us, event | category | flops | bytes accessed | tf_op | source)
XLA Modules:
  0.0 60.4 jit_solution(5815583372153912809)
XLA Ops:
  0.0 0.9 %convert_element_type.8 = bf16[343,2,32]{0,2,1:T(8,128)(2,1)S(1)} convert(f32[343,2,32]{0,2,1:T(8,128)} %param.13) | non-fusion elementwise | flops 21952 | bytes 131712 | tf_op jit(solution)/shard_map/convert_element_type | solution.py:310
  0.9 0.1 copy.18
  1.0 0.7 %pad.18.tr_ref = bf16[384,64]{1,0:T(8,128)(2,1)} pad(bf16[343,64]{1,0:T(8,128)(2,1)S(1)} %copy.18, bf16[]{:T(256)} %constant.73.clone.1), padding=0_41x0_0 | pad | bytes 93058 | tf_op jit(solution)/shard_map/jit(_pad)/pad | solution.py:310
  1.7 0.9 %copy.11 = s32[256,27]{1,0:T(8,128)S(1)} copy(s32[256,27]{0,1:T(8,128)} %param.11) | data formatting | bytes 55296 | tf_op args[4]
  2.6 0.3 fusion.5
  3.0 0.9 %copy.16 = s32[256,27]{1,0:T(8,128)S(1)} copy(s32[256,27]{0,1:T(8,128)} %param.12) | data formatting | bytes 55296 | tf_op args[5]
  3.9 0.1 pad_add_fusion
  4.0 0.7 %pad.17.idx_ref = s32[256,128]{1,0:T(8,128)} pad(s32[256,64]{1,0:T(8,128)S(1)} %pad_add_fusion, s32[]{:T(128)} %constant.63.clone.1), padding=0_0x0_64 | pad | bytes 196612 | tf_op jit(solution)/shard_map/jit(_pad)/pad | solution.py:308
  4.7 2.1 %fusion.13 = (f32[8,4096]{1,0:T(8,128)}, f32[8,4096]{1,0:T(8,128)}) fusion(f32[8,4096]{1,0:T(8,128)} %param.10), kind=kLoop, calls=%fused_computation.32 | loop fusion | bytes 393216 | tf_op jit(solution)/shard_map/sin | solution.py:355
  6.7 51.8 %shard_map.73 = bf16[256,1024]{1,0:T(8,128)(2,1)} custom-call(s32[16]{0:T(128)} %oct_ref.1, bf16[256,1024]{1,0:T(8,128)(2,1)} %bitcast.12, bf16[1024,4096]{1,0:T(8,128)(2,1)} %interp_ref.1, f32[8,4096]{1,0:T(8,128)} %get-tuple-element.6.cos_ref, f32[8,4096]{1,0:T(8,128)} %get-tuple-element.5.sin_ref, s32[256,128]{1,0:T(8,128)} %pad.17.idx_ref, ...), custom_call_target="tpu_custom_call" | custom-call | tf_op jit(solution)/shard_map/pallas_call | solution.py:314
  58.5 1.9 %copy.20 = bf16[16,2,8,1024]{3,2,1,0:T(8,128)(2,1)} copy(bf16[16,2,8,1024]{3,2,1,0:T(8,128)(2,1)} %bitcast.11) | data formatting | bytes 1048576
  (2 shorter events, 0.1 us)

commit v2 on v1

--- a/solution.py
+++ b/solution.py
@@ -32,8 +32,19 @@
     return xs
 
 
+def sincos(x):
+    n = jnp.floor(x * 0.6366197723675814 + 0.5)
+    r = x - n * 1.5703125 - n * 4.837512969970703125e-4 - n * 7.54978995489188216e-8
+    w = r * r
+    s = r + r * w * (-1.6666654611e-1 + w * (8.3321608736e-3 - w * 1.9515295891e-4))
+    c = 1.0 - 0.5 * w + w * w * (4.166664568298827e-2 + w * (-1.388731625493765e-3 + w * 2.443315711809948e-5))
+    odd, two = jnp.abs(n) == 1.0, jnp.abs(n) == 2.0
+    return jnp.where(odd, n * c, jnp.where(two, -s, s)), jnp.where(odd, -n * s, jnp.where(two, -c, c))
+
+
 def kernel(
-    oct_ref, leaf_ref, interp_ref, cos_ref, sin_ref, idx_ref, tr_ref, out_ref,
+    oct_ref, leaf_ref, interp_ref, angle_ref, partners_ref, types_ref, tr_ref, out_ref,
+    cos_ref, sin_ref, flat, idx, trp,
     interp_v, zsend, zrecv, ysend, arecv, idxall, oht, oh, fac, rsend, rrecv, xp, wsend, wrecv, shifted, acc,
     isem, zs, zr, ys, yr, xs_sem, xr_sem, rs, rr, ws, wr,
 ):
@@ -74,13 +85,16 @@
 
     lax.fori_loop(1, Z, greet_z, 0)
     lax.fori_loop(1, PLANE, greet_plane, 0)
-    pl.semaphore_wait(barrier, Z - 1 + PLANE - 1)
-
-    idx_copy = pltpu.make_async_remote_copy(
-        src_ref=idx_ref, dst_ref=idxall.at[box], send_sem=xs_sem, recv_sem=xr_sem,
-        device_id=(1 - box, d), device_id_type=MESH,
-    )
-    idx_copy.start()
+
+    for i in range(Z):
+        lanes = slice(i * CHUNK, (i + 1) * CHUNK)
+        sin_ref[:, lanes], cos_ref[:, lanes] = sincos(angle_ref[:, lanes])
+
+    def idx_copy(which, ref):
+        return pltpu.make_async_remote_copy(
+            src_ref=ref, dst_ref=idxall.at[box, which], send_sem=xs_sem.at[which], recv_sem=xr_sem.at[which],
+            device_id=(1 - box, d), device_id_type=MESH,
+        )
 
     def z_copy(src, dst, ssem, rsem, zc):
         return pltpu.make_async_remote_copy(
@@ -101,6 +115,15 @@
 
     def lift(i, carry):
         zc = order(i)
+        raise_plane(i, zc)
+
+        @pl.when(i < Z - 1)
+        def _():
+            z_copy(zsend, zrecv, zs, zr, zc).start()
+
+        return carry
+
+    def raise_plane(i, zc):
         fetch(i).wait()
         up = jnp.dot(leaf_ref[...], interp_v[zc], preferred_element_type=F32)
         parts = []
@@ -115,34 +138,59 @@
             parts += [real, imag]
         zsend[zc] = jnp.concatenate(parts, axis=0).astype(BF16)
 
-        @pl.when(i < Z - 1)
-        def _():
-            z_copy(zsend, zrecv, zs, zr, zc).start()
-
-        return carry
-
-    lax.fori_loop(0, Z, lift, 0)
+    first = order(0)
+    raise_plane(0, first)
+    pl.semaphore_wait(barrier, Z - 1 + PLANE - 1)
+    z_copy(zsend, zrecv, zs, zr, first).start()
+    idx_copy(0, partners_ref).start()
+    idx_copy(1, types_ref).start()
+    lax.fori_loop(1, Z, lift, 0)
     zrecv[z] = zsend[z]
 
-    idxall[box] = idx_ref[...]
     spread = (
         lax.broadcasted_iota(jnp.int32, (64, 256), 0)
         == lax.broadcasted_iota(jnp.int32, (64, 256), 1) // 128 * 32
         + box * WIDTH
         + lax.broadcasted_iota(jnp.int32, (64, 256), 1) % WIDTH
     )
-    table = jnp.dot(tr_ref[...], spread.astype(F32).astype(BF16), preferred_element_type=F32).astype(BF16)
-    idx_copy.wait()
+    trp[...] = jnp.zeros_like(trp)
+    trp[:, 0 : tr_ref.shape[1]] = tr_ref[...]
+    table = jnp.dot(
+        trp[...].T.astype(BF16), spread.astype(F32).astype(BF16), preferred_element_type=F32
+    ).astype(BF16)
+    idxall[box, 0] = partners_ref[...]
+    idxall[box, 1] = types_ref[...]
+    idx_copy(0, partners_ref).wait()
+    idx_copy(1, types_ref).wait()
+
+    p0 = lax.broadcasted_iota(jnp.int32, (256, 256), 0)
+    p1 = lax.broadcasted_iota(jnp.int32, (256, 256), 1)
+    place = (p1 == p0 // 2 % 8 * 32 + p0 // 16 * 2 + p0 % 2).astype(F32).astype(BF16)
+    nt = (((1,), (1,)), ((), ()))
+    flat[...] = jnp.zeros_like(flat)
+    for group in range(2):
+        p, t = idxall[group, 0], idxall[group, 1]
+        high = (p // 256 * 16 + p // 2 % 16) * 16
+        flat[0, 0:LINKED] = high.astype(F32)
+        flat[0, 32 : 32 + LINKED] = (t // 16 * 16).astype(F32)
+        flat[1, 0:LINKED] = (p // 32 % 8 * 2 + p % 2).astype(F32)
+        flat[1, 32 : 32 + LINKED] = (t % 16).astype(F32)
+        index = lax.dot_general(place, flat[0].astype(BF16), nt, preferred_element_type=F32)
+        index += lax.dot_general(place, flat[1].astype(BF16), nt, preferred_element_type=F32)
+        idx[group] = index
 
     def indices(pb):
         half = BLOCKS // 2
-        return idxall[pb // half, pl.ds(pl.multiple_of(pb % half * PB, PB), PB), :]
+        return idx[pb // half, pl.ds(pl.multiple_of(pb % half * PB, PB), PB), :]
+
+    def hot(index, at, lanes):
+        wide = lax.broadcasted_iota(jnp.int32, (PB, lanes), 1).astype(F32)
+        return (wide == index[:, at : at + 1]).astype(F32).astype(BF16)
 
     def factors(pb, carry):
         index = indices(pb)
-        wide = lax.broadcasted_iota(jnp.int32, (PB, TYPES), 1)
         for k in range(LINKED):
-            oht[k * PB : (k + 1) * PB, :] = (wide == index[:, 32 + k : 33 + k]).astype(F32).astype(BF16)
+            oht[k * PB : (k + 1) * PB, :] = hot(index, 32 + k, TYPES)
         fac[pb] = jnp.dot(oht[...], table, preferred_element_type=F32)
         return carry
 
@@ -187,9 +235,8 @@
 
     def sources(pb, carry):
         index = indices(pb)
-        wide = lax.broadcasted_iota(jnp.int32, (PB, 512), 1)
         for k in range(LINKED):
-            oh[pb, k * PB : (k + 1) * PB, :] = (wide == index[:, k : k + 1]).astype(F32).astype(BF16)
+            oh[pb, k * PB : (k + 1) * PB, :] = hot(index, k, 512)
         return carry
 
     lax.fori_loop(0, BLOCKS, sources, 0)
@@ -212,7 +259,8 @@
             device_id=plane_of_spot(t), device_id_type=MESH,
         )
 
-    def translate(pb, carry):
+    def translate(i, carry):
+        pb = (slab * 16 // PB + 1 + i) % BLOCKS
         got = jnp.dot(oh[pb], arecv[...].reshape(512, 256), preferred_element_type=F32)
         real = imag = None
         for k in range(LINKED):
@@ -298,16 +346,8 @@
 def local(leaf_patterns, octant, interp, shift_angle, partners, types, translators):
     boxes, pairs, excite, low = leaf_patterns.shape
     high = interp.shape[1]
-    own = partners.shape[0]
-    place = (partners // 256 * 16 + partners // 2 % 16) * 16 + partners // 32 % 8 * 2 + partners % 2
-
-    def lay(x):
-        x = x.reshape(Z, own // Z // 2, 2, LINKED).transpose(1, 0, 2, 3).reshape(own, LINKED)
-        return jnp.pad(x, ((0, 0), (0, 32 - LINKED)))
-
-    index = jnp.pad(jnp.concatenate([lay(place), lay(types)], axis=1), ((0, 0), (0, 64)))
+    linked, own = partners.shape[1], partners.shape[0]
     offsets = translators.shape[0]
-    tr = jnp.pad(translators.reshape(offsets, -1).astype(BF16), ((0, TYPES - offsets), (0, 0)))
     rows = boxes * pairs * excite
     vmem = pl.BlockSpec(memory_space=pltpu.VMEM)
     dma = pltpu.SemaphoreType.DMA
@@ -325,12 +365,17 @@
         ],
         out_specs=vmem,
         scratch_shapes=[
+            pltpu.VMEM((8, high), F32),
+            pltpu.VMEM((8, high), F32),
+            pltpu.VMEM((2, 128, own), F32),
+            pltpu.VMEM((2, own, 128), F32),
+            pltpu.VMEM((64, TYPES), F32),
             pltpu.VMEM((Z, low, CHUNK), BF16),
             pltpu.VMEM((Z, 32, CHUNK), BF16),
             pltpu.VMEM((Z, 32, CHUNK), BF16),
             pltpu.VMEM((PLANE, 16, 256), BF16),
             pltpu.VMEM((PLANE, 16, 256), BF16),
-            pltpu.VMEM((2, own, 128), jnp.int32),
+            pltpu.VMEM((2, 2, linked, own), jnp.int32),
             pltpu.VMEM((ROWS, TYPES), BF16),
             pltpu.VMEM((BLOCKS, ROWS, 512), BF16),
             pltpu.VMEM((BLOCKS, ROWS, 256), F32),
@@ -341,20 +386,20 @@
             pltpu.VMEM((Z, 32, CHUNK), BF16),
             pltpu.VMEM((rows, CHUNK), BF16),
             pltpu.VMEM((rows, low), F32),
-            dma((Z,)), dma((Z,)), dma((Z,)), dma((PLANE,)), dma((PLANE,)), dma, dma,
+            dma((Z,)), dma((Z,)), dma((Z,)), dma((PLANE,)), dma((PLANE,)), dma((2,)), dma((2,)),
             dma((PLANE,)), dma((PLANE,)), dma((Z,)), dma((Z,)),
         ],
         compiler_params=pltpu.CompilerParams(
-            collective_id=0, has_side_effects=True, vmem_limit_bytes=60 * 1024 * 1024
+            collective_id=0, has_side_effects=True, vmem_limit_bytes=58 * 1024 * 1024
         ),
     )(
         octant,
         leaf_patterns.reshape(rows, low),
         interp,
-        jnp.cos(shift_angle),
-        jnp.sin(shift_angle),
-        index,
-        tr,
+        shift_angle,
+        partners.T,
+        types.T,
+        translators.transpose(1, 2, 0).reshape(-1, offsets),
     )
     return out.reshape(boxes, pairs, excite, low)
 

time: 60.7 us -> 54.1 us (0.89)
  the two profiles are of different devices: /device:TPU:13 before, /device:TPU:1 now
where the time goes in v2:
time: 54.1 us; the launch traced here: 54 us
  Pallas kernels  52.1 us (96%)
  local copies, waits for them, and re-layouts  1.88 us (3%)
    pallas_call x1, Pallas kernels, local(): pl.pallas_call(kernel, out_shape=jax.ShapeDtypeStruct((rows, low), BF16),...  52.1 us
    unnamed x1, local copies, waits for them, and re-layouts  1.88 us

profile of v2, /device:TPU:1, one launch (start us, length us, event | category | flops | bytes accessed | tf_op | source)
XLA Modules:
  0.0 54.0 jit_solution(745437496760576332)
XLA Ops:
  0.0 52.1 %shard_map.73 = bf16[256,1024]{1,0:T(8,128)(2,1)} custom-call(s32[16]{0:T(128)} %oct_ref.1, bf16[256,1024]{1,0:T(8,128)(2,1)} %bitcast.8, bf16[1024,4096]{1,0:T(8,128)(2,1)} %interp_ref.1, f32[8,4096]{1,0:T(8,128)} %angle_ref.1, s32[27,256]{1,0:T(8,128)} %bitcast.10, s32[27,256]{1,0:T(8,128)} %bitcast.11, f32[64,343]{1,0:T(8,128)} %bitcast.9), custom_call_target="tpu_custom_call" | custom-call | tf_op jit(solution)/shard_map/pallas_call | solution.py:354
  52.1 1.9 %copy.9 = bf16[16,2,8,1024]{3,2,1,0:T(8,128)(2,1)} copy(bf16[16,2,8,1024]{3,2,1,0:T(8,128)(2,1)} %bitcast.7) | data formatting | bytes 1048576

commit v3 on v2

--- a/solution.py
+++ b/solution.py
@@ -10,6 +10,7 @@
 PLANE = 32
 WIDTH = 16
 CHUNK = PLANE * WIDTH
+HALF = CHUNK // 2
 PB = 64
 LINKED = 27
 ROWS = PB * LINKED
@@ -43,7 +44,8 @@
 
 
 def kernel(
-    oct_ref, leaf_ref, interp_ref, angle_ref, partners_ref, types_ref, tr_ref, out_ref,
+    oct_ref, leaf_hbm, interp_ref, angle_hbm, partners_hbm, types_hbm, tr_hbm, out_ref,
+    leaf_ref, angle_ref, partners_ref, types_ref, tr_ref, in_sem,
     cos_ref, sin_ref, flat, idx, trp,
     interp_v, zsend, zrecv, ysend, arecv, idxall, oht, oh, fac, rsend, rrecv, xp, wsend, wrecv, shifted, acc,
     isem, zs, zr, ys, yr, xs_sem, xr_sem, rs, rr, ws, wr,
@@ -65,13 +67,27 @@
         half = (i + 1) // 2
         return (z + 4 + half * (1 - 2 * (i % 2))) % 8
 
-    def fetch(i):
-        zc = order(i)
-        at = pl.multiple_of(zc * CHUNK, CHUNK)
-        return pltpu.make_async_copy(interp_ref.at[:, pl.ds(at, CHUNK)], interp_v.at[zc], isem.at[i])
-
-    for i in range(Z):
+    def half(j):
+        return (yxc // 8 + 1 + j) % 2
+
+    def fetch(n):
+        h, zc = half(n // Z), order(n % Z)
+        at = pl.multiple_of(zc * CHUNK + h * HALF, HALF)
+        return pltpu.make_async_copy(interp_ref.at[:, pl.ds(at, HALF)], interp_v.at[zc, h], isem.at[n])
+
+    angle_in = pltpu.make_async_copy(angle_hbm, angle_ref, in_sem.at[0])
+    leaf_in = pltpu.make_async_copy(leaf_hbm, leaf_ref, in_sem.at[1])
+    partners_in = pltpu.make_async_copy(partners_hbm, partners_ref, in_sem.at[2])
+    types_in = pltpu.make_async_copy(types_hbm, types_ref, in_sem.at[3])
+    tr_in = pltpu.make_async_copy(tr_hbm, tr_ref, in_sem.at[4])
+    angle_in.start()
+    leaf_in.start()
+    fetch(0).start()
+    partners_in.start()
+    types_in.start()
+    for i in range(1, 2 * Z):
         fetch(i).start()
+    tr_in.start()
 
     barrier = pltpu.get_barrier_semaphore()
 
@@ -86,6 +102,7 @@
     lax.fori_loop(1, Z, greet_z, 0)
     lax.fori_loop(1, PLANE, greet_plane, 0)
 
+    angle_in.wait()
     for i in range(Z):
         lanes = slice(i * CHUNK, (i + 1) * CHUNK)
         sin_ref[:, lanes], cos_ref[:, lanes] = sincos(angle_ref[:, lanes])
@@ -96,56 +113,59 @@
             device_id=(1 - box, d), device_id_type=MESH,
         )
 
-    def z_copy(src, dst, ssem, rsem, zc):
-        return pltpu.make_async_remote_copy(
-            src_ref=src.at[zc], dst_ref=dst.at[z], send_sem=ssem.at[zc], recv_sem=rsem.at[z],
+    def z_copy(src, dst, ssem, rsem, h, zc):
+        return pltpu.make_async_remote_copy(
+            src_ref=src.at[h, zc], dst_ref=dst.at[h, z], send_sem=ssem.at[h, zc], recv_sem=rsem.at[h, z],
             device_id=(box, zc * 16 + yxc), device_id_type=MESH,
         )
 
-    def z_arrival(src, dst, ssem, rsem, zc):
-        return pltpu.make_async_remote_copy(
-            src_ref=src.at[zc], dst_ref=dst.at[zc], send_sem=ssem.at[zc], recv_sem=rsem.at[zc],
+    def z_arrival(src, dst, ssem, rsem, h, zc):
+        return pltpu.make_async_remote_copy(
+            src_ref=src.at[h, zc], dst_ref=dst.at[h, zc], send_sem=ssem.at[h, zc], recv_sem=rsem.at[h, zc],
             device_id=(box, zc * 16 + yxc), device_id_type=MESH,
         )
 
-    def phases(child, zc):
+    def phases(child, h, zc):
         o = oct_ref[child]
-        at = pl.ds(pl.multiple_of(zc * CHUNK, CHUNK), CHUNK)
+        at = pl.ds(pl.multiple_of(zc * CHUNK + h * HALF, HALF), HALF)
         return cos_ref[pl.ds(o, 1), at], sin_ref[pl.ds(o, 1), at]
 
-    def lift(i, carry):
-        zc = order(i)
-        raise_plane(i, zc)
-
-        @pl.when(i < Z - 1)
+    def lift(n, carry):
+        h, zc = half(n // Z), order(n % Z)
+        raise_plane(n, h, zc)
+
+        @pl.when(n % Z < Z - 1)
         def _():
-            z_copy(zsend, zrecv, zs, zr, zc).start()
-
-        return carry
-
-    def raise_plane(i, zc):
-        fetch(i).wait()
-        up = jnp.dot(leaf_ref[...], interp_v[zc], preferred_element_type=F32)
+            z_copy(zsend, zrecv, zs, zr, h, zc).start()
+
+        return carry
+
+    def raise_plane(n, h, zc):
+        fetch(n).wait()
+        up = jnp.dot(leaf_ref[...], interp_v[zc, h], preferred_element_type=F32)
         parts = []
         for parent in range(2):
             real = imag = None
             for k in range(8):
                 child = parent * 8 + k
-                cs, sn = phases(child, zc)
+                cs, sn = phases(child, h, zc)
                 ur, ui = up[child * 16 : child * 16 + 8], up[child * 16 + 8 : child * 16 + 16]
                 a, b = ur * cs - ui * sn, ur * sn + ui * cs
                 real, imag = (a, b) if real is None else (real + a, imag + b)
             parts += [real, imag]
-        zsend[zc] = jnp.concatenate(parts, axis=0).astype(BF16)
-
-    first = order(0)
-    raise_plane(0, first)
+        zsend[h, zc] = jnp.concatenate(parts, axis=0).astype(BF16)
+
+    leaf_in.wait()
+    raise_plane(0, half(0), order(0))
     pl.semaphore_wait(barrier, Z - 1 + PLANE - 1)
-    z_copy(zsend, zrecv, zs, zr, first).start()
+    z_copy(zsend, zrecv, zs, zr, half(0), order(0)).start()
+    partners_in.wait()
+    types_in.wait()
     idx_copy(0, partners_ref).start()
     idx_copy(1, types_ref).start()
-    lax.fori_loop(1, Z, lift, 0)
-    zrecv[z] = zsend[z]
+    lax.fori_loop(1, 2 * Z, lift, 0)
+    for h in range(2):
+        zrecv[h, z] = zsend[h, z]
 
     spread = (
         lax.broadcasted_iota(jnp.int32, (64, 256), 0)
@@ -153,6 +173,7 @@
         + box * WIDTH
         + lax.broadcasted_iota(jnp.int32, (64, 256), 1) % WIDTH
     )
+    tr_in.wait()
     trp[...] = jnp.zeros_like(trp)
     trp[:, 0 : tr_ref.shape[1]] = tr_ref[...]
     table = jnp.dot(
@@ -194,25 +215,25 @@
         fac[pb] = jnp.dot(oht[...], table, preferred_element_type=F32)
         return carry
 
-    lax.fori_loop(0, BLOCKS, factors, 0)
-
-    def z_wait(i, carry):
-        zc = (z + i) % 8
-        z_arrival(zsend, zrecv, zs, zr, zc).wait_recv()
-        return carry
-
-    lax.fori_loop(1, Z, z_wait, 0)
+    def z_wait(h):
+        def wait(i, carry):
+            z_arrival(zsend, zrecv, zs, zr, h, (z + i) % 8).wait_recv()
+            return carry
+
+        lax.fori_loop(1, Z, wait, 0)
 
     r0 = lax.broadcasted_iota(jnp.int32, (256, 256), 0)
     r1 = lax.broadcasted_iota(jnp.int32, (256, 256), 1)
     turn = (r1 == r0 % 16 * 16 + r0 // 16).astype(F32).astype(BF16)
-    turned = jnp.dot(turn, zrecv[...].reshape(256, CHUNK), preferred_element_type=F32)
-    for pair in range(2):
-        for dh in range(4):
-            lanes = slice(dh * 128, dh * 128 + 128)
-            blocks = [turned[(pair * 8 + j) * 16 : (pair * 8 + j) * 16 + 16, lanes] for j in range(8)]
-            for j, y in enumerate(block_transpose(blocks)):
-                ysend[dh * 8 + j, :, pair * 128 : pair * 128 + 128] = y.astype(BF16)
+
+    def regroup(h):
+        turned = jnp.dot(turn, zrecv[h].reshape(256, HALF), preferred_element_type=F32)
+        for pair in range(2):
+            for dh in range(2):
+                lanes = slice(dh * 128, dh * 128 + 128)
+                blocks = [turned[(pair * 8 + j) * 16 : (pair * 8 + j) * 16 + 16, lanes] for j in range(8)]
+                for j, y in enumerate(block_transpose(blocks)):
+                    ysend[h * 16 + dh * 8 + j, :, pair * 128 : pair * 128 + 128] = y.astype(BF16)
 
     def y_copy(t):
         return pltpu.make_async_remote_copy(
@@ -226,12 +247,23 @@
             device_id=plane_of_slab(s), device_id_type=MESH,
         )
 
-    def y_start(i, carry):
-        y_copy((spot + i) % PLANE).start()
-        return carry
-
-    lax.fori_loop(1, PLANE, y_start, 0)
+    def y_start(h):
+        def start(i, carry):
+            y_copy(h * 16 + (spot + i) % 16).start()
+            return carry
+
+        return start
+
+    lax.fori_loop(0, 1, factors, 0)
+    z_wait(half(0))
+    regroup(half(0))
+    lax.fori_loop(0, 16, y_start(half(0)), 0)
+    lax.fori_loop(1, 5, factors, 0)
+    z_wait(half(1))
+    regroup(half(1))
+    lax.fori_loop(1, 16, y_start(half(1)), 0)
     arecv[slab] = ysend[spot]
+    lax.fori_loop(5, BLOCKS, factors, 0)
 
     def sources(pb, carry):
         index = indices(pb)
@@ -260,7 +292,10 @@
         )
 
     def translate(i, carry):
-        pb = (slab * 16 // PB + 1 + i) % BLOCKS
+        y = yxc // 4
+        across = (1 - y // 2) * 2 + (y + i // 2) % 2
+        near = y // 2 * 2 + (y + 1 - (i // 2) % 2) % 2
+        pb = (box + 1 + i) % 2 * 4 + across + (near - across) * (i // 4)
         got = jnp.dot(oh[pb], arecv[...].reshape(512, 256), preferred_element_type=F32)
         real = imag = None
         for k in range(LINKED):
@@ -280,58 +315,75 @@
 
         return carry
 
-    lax.fori_loop(0, BLOCKS, translate, 0)
+    def r_wait(h, first):
+        def wait(i, carry):
+            r_arrival(h * 16 + (spot + i) % 16).wait_recv()
+            return carry
+
+        lax.fori_loop(first, 16, wait, 0)
+
+    def ungroup(h):
+        for pair in range(2):
+            for dh in range(2):
+                lanes = slice(dh * 128, dh * 128 + 128)
+                blocks = [
+                    rrecv[h * 16 + dh * 8 + j, :, pair * 128 : pair * 128 + 128].astype(F32) for j in range(8)
+                ]
+                for j, y in enumerate(block_transpose(blocks)):
+                    xp[(pair * 8 + j) * 16 : (pair * 8 + j) * 16 + 16, lanes] = y.astype(BF16)
+        wsend[h] = jnp.dot(turn, xp[...], preferred_element_type=F32).astype(BF16).reshape(Z, 32, HALF)
+
+    def w_start(h):
+        def start(i, carry):
+            z_copy(wsend, wrecv, ws, wr, h, order(i)).start()
+            return carry
+
+        lax.fori_loop(0, Z - 1, start, 0)
+
+    lax.fori_loop(0, 6, translate, 0)
+    r_wait(half(0), 0)
+    ungroup(half(0))
+    w_start(half(0))
+    lax.fori_loop(6, BLOCKS, translate, 0)
     rrecv[spot] = rsend[slab]
-
-    def r_wait(i, carry):
-        r_arrival((spot + i) % PLANE).wait_recv()
-        return carry
-
-    lax.fori_loop(1, PLANE, r_wait, 0)
-
-    for pair in range(2):
-        for dh in range(4):
-            lanes = slice(dh * 128, dh * 128 + 128)
-            blocks = [rrecv[dh * 8 + j, :, pair * 128 : pair * 128 + 128].astype(F32) for j in range(8)]
-            for j, y in enumerate(block_transpose(blocks)):
-                xp[(pair * 8 + j) * 16 : (pair * 8 + j) * 16 + 16, lanes] = y.astype(BF16)
-    wsend[...] = jnp.dot(turn, xp[...], preferred_element_type=F32).astype(BF16).reshape(Z, 32, CHUNK)
-
-    def w_start(i, carry):
-        z_copy(wsend, wrecv, ws, wr, order(i)).start()
-        return carry
-
-    lax.fori_loop(0, Z - 1, w_start, 0)
-    wrecv[z] = wsend[z]
+    r_wait(half(1), 1)
+    ungroup(half(1))
+    w_start(half(1))
+    for h in range(2):
+        wrecv[h, z] = wsend[h, z]
     acc[...] = jnp.zeros_like(acc)
 
-    def descend(i, carry):
-        zc = order(Z - 1 - i)
-
-        @pl.when(i > 0)
-        def _():
-            z_arrival(wsend, wrecv, ws, wr, zc).wait_recv()
-
-        got = wrecv[zc].astype(F32)
-        for parent in range(2):
-            re, im = got[parent * 16 : parent * 16 + 8], got[parent * 16 + 8 : parent * 16 + 16]
-            for k in range(8):
-                child = parent * 8 + k
-                cs, sn = phases(child, zc)
-                both = jnp.concatenate([re * cs + im * sn, im * cs - re * sn], axis=0)
-                shifted[child * 16 : child * 16 + 16, :] = both.astype(BF16)
-        acc[...] += lax.dot_general(
-            shifted[...], interp_v[zc], (((1,), (1,)), ((), ())), preferred_element_type=F32
-        )
+    def descend(n, carry):
+        terms = []
+        for part in range(2):
+            i = n % (Z // 2) * 2 + part
+            h, zc = half(n // (Z // 2)), order(Z - 1 - i)
+
+            @pl.when(i > 0)
+            def _():
+                z_arrival(wsend, wrecv, ws, wr, h, zc).wait_recv()
+
+            got = wrecv[h, zc].astype(F32)
+            for parent in range(2):
+                re, im = got[parent * 16 : parent * 16 + 8], got[parent * 16 + 8 : parent * 16 + 16]
+                for k in range(8):
+                    child = parent * 8 + k
+                    cs, sn = phases(child, h, zc)
+                    both = jnp.concatenate([re * cs + im * sn, im * cs - re * sn], axis=0)
+                    shifted[part, child * 16 : child * 16 + 16, :] = both.astype(BF16)
+            terms.append(
+                lax.dot_general(shifted[part], interp_v[zc, h], nt, preferred_element_type=F32)
+            )
+        acc[...] += terms[0] + terms[1]
         return carry
 
     lax.fori_loop(0, Z, descend, 0)
     out_ref[...] = (acc[...] * 0.25).astype(BF16)
 
     def z_sent(i, carry):
-        zc = (z + i) % 8
-        z_copy(zsend, zrecv, zs, zr, zc).wait_send()
-        z_copy(wsend, wrecv, ws, wr, zc).wait_send()
+        for h in range(2):
+            z_copy(zsend, zrecv, zs, zr, h, (z + i) % 8).wait_send()
+            z_copy(wsend, wrecv, ws, wr, h, (z + i) % 8).wait_send()
         return carry
 
     def plane_sent(i, carry):
@@ -354,25 +406,23 @@
     out = pl.pallas_call(
         kernel,
         out_shape=jax.ShapeDtypeStruct((rows, low), BF16),
-        in_specs=[
-            pl.BlockSpec(memory_space=pltpu.SMEM),
-            vmem,
-            pl.BlockSpec(memory_space=pl.ANY),
-            vmem,
-            vmem,
-            vmem,
-            vmem,
-        ],
+        in_specs=[pl.BlockSpec(memory_space=pltpu.SMEM)] + [pl.BlockSpec(memory_space=pltpu.HBM)] * 6,
         out_specs=vmem,
         scratch_shapes=[
+            pltpu.VMEM((rows, low), BF16),
+            pltpu.VMEM((8, high), F32),
+            pltpu.VMEM((linked, own), jnp.int32),
+            pltpu.VMEM((linked, own), jnp.int32),
+            pltpu.VMEM((64, offsets), F32),
+            dma((5,)),
             pltpu.VMEM((8, high), F32),
             pltpu.VMEM((8, high), F32),
             pltpu.VMEM((2, 128, own), F32),
             pltpu.VMEM((2, own, 128), F32),
             pltpu.VMEM((64, TYPES), F32),
-            pltpu.VMEM((Z, low, CHUNK), BF16),
-            pltpu.VMEM((Z, 32, CHUNK), BF16),
-            pltpu.VMEM((Z, 32, CHUNK), BF16),
+            pltpu.VMEM((Z, 2, low, HALF), BF16),
+            pltpu.VMEM((2, Z, 32, HALF), BF16),
+            pltpu.VMEM((2, Z, 32, HALF), BF16),
             pltpu.VMEM((PLANE, 16, 256), BF16),
             pltpu.VMEM((PLANE, 16, 256), BF16),
             pltpu.VMEM((2, 2, linked, own), jnp.int32),
@@ -381,13 +431,13 @@
             pltpu.VMEM((BLOCKS, ROWS, 256), F32),
             pltpu.VMEM((PLANE, 16, 256), BF16),
             pltpu.VMEM((PLANE, 16, 256), BF16),
-            pltpu.VMEM((256, CHUNK), BF16),
-            pltpu.VMEM((Z, 32, CHUNK), BF16),
-            pltpu.VMEM((Z, 32, CHUNK), BF16),
-            pltpu.VMEM((rows, CHUNK), BF16),
+            pltpu.VMEM((256, HALF), BF16),
+            pltpu.VMEM((2, Z, 32, HALF), BF16),
+            pltpu.VMEM((2, Z, 32, HALF), BF16),
+            pltpu.VMEM((2, rows, HALF), BF16),
             pltpu.VMEM((rows, low), F32),
-            dma((Z,)), dma((Z,)), dma((Z,)), dma((PLANE,)), dma((PLANE,)), dma((2,)), dma((2,)),
-            dma((PLANE,)), dma((PLANE,)), dma((Z,)), dma((Z,)),
+            dma((2 * Z,)), dma((2, Z)), dma((2, Z)), dma((PLANE,)), dma((PLANE,)), dma((2,)), dma((2,)),
+            dma((PLANE,)), dma((PLANE,)), dma((2, Z)), dma((2, Z)),
         ],
         compiler_params=pltpu.CompilerParams(
             collective_id=0, has_side_effects=True, vmem_limit_bytes=58 * 1024 * 1024

time: 54.1 us -> 52.7 us (0.974)
  Pallas kernels: 52.1 us -> 50.7 us
    pallas_call x1, Pallas kernels: 52.1 us -> 50.7 us  [local(): pl.pallas_call(kernel, out_shape=jax.ShapeDtypeStruct((rows, low), BF16),...]
where the time goes in v3:
time: 52.7 us; the launch traced here: 52.6 us
  Pallas kernels  50.7 us (96%)
  local copies, waits for them, and re-layouts  1.88 us (4%)
    pallas_call x1, Pallas kernels, local(): pl.pallas_call(kernel, out_shape=jax.ShapeDtypeStruct((rows, low), BF16),...  50.7 us
    unnamed x1, local copies, waits for them, and re-layouts  1.88 us

profile of v3, /device:TPU:1, one launch (start us, length us, event | category | flops | bytes accessed | tf_op | source)
XLA Modules:
  0.0 52.6 jit_solution(12420670297324938879)
XLA Ops:
  0.0 50.7 %shard_map.73 = bf16[256,1024]{1,0:T(8,128)(2,1)} custom-call(s32[16]{0:T(128)} %oct_ref.1, bf16[256,1024]{1,0:T(8,128)(2,1)} %bitcast.8, bf16[1024,4096]{1,0:T(8,128)(2,1)} %interp_ref.1, f32[8,4096]{1,0:T(8,128)} %angle_hbm.1, s32[27,256]{1,0:T(8,128)} %bitcast.10, s32[27,256]{1,0:T(8,128)} %bitcast.11, f32[64,343]{1,0:T(8,128)} %bitcast.9), custom_call_target="tpu_custom_call" | custom-call | tf_op jit(solution)/shard_map/pallas_call | solution.py:406
  50.7 1.9 %copy.9 = bf16[16,2,8,1024]{3,2,1,0:T(8,128)(2,1)} copy(bf16[16,2,8,1024]{3,2,1,0:T(8,128)(2,1)} %bitcast.7) | data formatting | bytes 1048576

commit v4 on v3

--- a/solution.py
+++ b/solution.py
@@ -57,21 +57,17 @@
     slab = box * 16 + yxc
     spot = yxc * 2 + box
 
-    def plane_of_slab(s):
-        return (s // 16, z * 16 + s % 16)
-
-    def plane_of_spot(t):
-        return (t % 2, z * 16 + t // 2)
+    def wrap(x, n):
+        return jnp.where(x >= n, x - n, x)
 
     def order(i):
-        half = (i + 1) // 2
-        return (z + 4 + half * (1 - 2 * (i % 2))) % 8
+        return lax.rem(z + 4 + lax.div(i + 1, 2) * (1 - 2 * lax.rem(i, 2)), 8)
 
     def half(j):
-        return (yxc // 8 + 1 + j) % 2
+        return lax.rem(yxc // 8 + 1 + j, 2)
 
     def fetch(n):
-        h, zc = half(n // Z), order(n % Z)
+        h, zc = half(lax.div(n, Z)), order(lax.rem(n, Z))
         at = pl.multiple_of(zc * CHUNK + h * HALF, HALF)
         return pltpu.make_async_copy(interp_ref.at[:, pl.ds(at, HALF)], interp_v.at[zc, h], isem.at[n])
 
@@ -91,16 +87,26 @@
 
     barrier = pltpu.get_barrier_semaphore()
 
+    def greet(device):
+        pl.semaphore_signal(barrier, inc=1, device_id=device, device_id_type=MESH)
+
     def greet_z(i, carry):
-        pl.semaphore_signal(barrier, inc=1, device_id=(box, (z + i) % 8 * 16 + yxc), device_id_type=MESH)
+        greet((box, wrap(z + i, Z) * 16 + yxc))
         return carry
 
     def greet_plane(i, carry):
-        pl.semaphore_signal(barrier, inc=1, device_id=plane_of_slab((slab + i) % PLANE), device_id_type=MESH)
+        for group in range(2):
+            greet((group, z * 16 + wrap(yxc + i, 16)))
         return carry
 
     lax.fori_loop(1, Z, greet_z, 0)
-    lax.fori_loop(1, PLANE, greet_plane, 0)
+    greet((1 - box, d))
+    lax.fori_loop(1, 16, greet_plane, 0)
+
+    def many(src, dst, ssem, rsem):
+        return pltpu.make_async_remote_copy(
+            src_ref=src, dst_ref=dst, send_sem=ssem, recv_sem=rsem, device_id=(1 - box, d), device_id_type=MESH
+        )
 
     angle_in.wait()
     for i in range(Z):
@@ -115,13 +121,7 @@
 
     def z_copy(src, dst, ssem, rsem, h, zc):
         return pltpu.make_async_remote_copy(
-            src_ref=src.at[h, zc], dst_ref=dst.at[h, z], send_sem=ssem.at[h, zc], recv_sem=rsem.at[h, z],
-            device_id=(box, zc * 16 + yxc), device_id_type=MESH,
-        )
-
-    def z_arrival(src, dst, ssem, rsem, h, zc):
-        return pltpu.make_async_remote_copy(
-            src_ref=src.at[h, zc], dst_ref=dst.at[h, zc], send_sem=ssem.at[h, zc], recv_sem=rsem.at[h, zc],
+            src_ref=src.at[h, zc], dst_ref=dst.at[h, z], send_sem=ssem.at[h], recv_sem=rsem,
             device_id=(box, zc * 16 + yxc), device_id_type=MESH,
         )
 
@@ -131,12 +131,12 @@
         return cos_ref[pl.ds(o, 1), at], sin_ref[pl.ds(o, 1), at]
 
     def lift(n, carry):
-        h, zc = half(n // Z), order(n % Z)
+        h, zc = half(lax.div(n, Z)), order(lax.rem(n, Z))
         raise_plane(n, h, zc)
 
-        @pl.when(n % Z < Z - 1)
+        @pl.when(lax.rem(n, Z) < Z - 1)
         def _():
-            z_copy(zsend, zrecv, zs, zr, h, zc).start()
+            z_copy(zsend, zrecv, zs, zr.at[h], h, zc).start()
 
         return carry
 
@@ -156,9 +156,9 @@
         zsend[h, zc] = jnp.concatenate(parts, axis=0).astype(BF16)
 
     leaf_in.wait()
-    raise_plane(0, half(0), order(0))
+    raise_plane(0, half(0), order(jnp.int32(0)))
     pl.semaphore_wait(barrier, Z - 1 + PLANE - 1)
-    z_copy(zsend, zrecv, zs, zr, half(0), order(0)).start()
+    z_copy(zsend, zrecv, zs, zr.at[half(0)], half(0), order(jnp.int32(0))).start()
     partners_in.wait()
     types_in.wait()
     idx_copy(0, partners_ref).start()
@@ -215,12 +215,9 @@
         fac[pb] = jnp.dot(oht[...], table, preferred_element_type=F32)
         return carry
 
-    def z_wait(h):
-        def wait(i, carry):
-            z_arrival(zsend, zrecv, zs, zr, h, (z + i) % 8).wait_recv()
-            return carry
-
-        lax.fori_loop(1, Z, wait, 0)
+    def z_all(h):
+        most = (h, pl.ds(0, Z - 1))
+        return many(zsend.at[most], zrecv.at[most], zs.at[h], zr.at[h])
 
     r0 = lax.broadcasted_iota(jnp.int32, (256, 256), 0)
     r1 = lax.broadcasted_iota(jnp.int32, (256, 256), 1)
@@ -235,33 +232,30 @@
                 for j, y in enumerate(block_transpose(blocks)):
                     ysend[h * 16 + dh * 8 + j, :, pair * 128 : pair * 128 + 128] = y.astype(BF16)
 
-    def y_copy(t):
-        return pltpu.make_async_remote_copy(
-            src_ref=ysend.at[t], dst_ref=arecv.at[slab], send_sem=ys.at[t], recv_sem=yr.at[slab],
-            device_id=plane_of_spot(t), device_id_type=MESH,
-        )
-
-    def y_arrival(s):
-        return pltpu.make_async_remote_copy(
-            src_ref=ysend.at[s], dst_ref=arecv.at[s], send_sem=ys.at[s], recv_sem=yr.at[s],
-            device_id=plane_of_slab(s), device_id_type=MESH,
-        )
-
-    def y_start(h):
+    def y_start(group, place):
+        t = place * 2 + group
+        pltpu.make_async_remote_copy(
+            src_ref=ysend.at[t], dst_ref=arecv.at[slab], send_sem=ys, recv_sem=yr,
+            device_id=(group, z * 16 + place), device_id_type=MESH,
+        ).start()
+
+    def y_starts(h):
         def start(i, carry):
-            y_copy(h * 16 + (spot + i) % 16).start()
+            for group in range(2):
+                y_start(group, h * 8 + wrap(yxc % 8 + i, 8))
             return carry
 
         return start
 
     lax.fori_loop(0, 1, factors, 0)
-    z_wait(half(0))
+    z_all(half(0)).wait_recv()
     regroup(half(0))
-    lax.fori_loop(0, 16, y_start(half(0)), 0)
+    lax.fori_loop(0, 8, y_starts(half(0)), 0)
     lax.fori_loop(1, 5, factors, 0)
-    z_wait(half(1))
+    z_all(half(1)).wait_recv()
     regroup(half(1))
-    lax.fori_loop(1, 16, y_start(half(1)), 0)
+    y_start(1 - box, yxc)
+    lax.fori_loop(1, 8, y_starts(half(1)), 0)
     arecv[slab] = ysend[spot]
     lax.fori_loop(5, BLOCKS, factors, 0)
 
@@ -273,29 +267,17 @@
 
     lax.fori_loop(0, BLOCKS, sources, 0)
 
-    def y_wait(i, carry):
-        y_arrival((slab + i) % PLANE).wait_recv()
-        return carry
-
-    lax.fori_loop(1, PLANE, y_wait, 0)
-
-    def r_copy(s):
-        return pltpu.make_async_remote_copy(
-            src_ref=rsend.at[s], dst_ref=rrecv.at[spot], send_sem=rs.at[s], recv_sem=rr.at[spot],
-            device_id=plane_of_slab(s), device_id_type=MESH,
-        )
-
-    def r_arrival(t):
-        return pltpu.make_async_remote_copy(
-            src_ref=rsend.at[t], dst_ref=rrecv.at[t], send_sem=rs.at[t], recv_sem=rr.at[t],
-            device_id=plane_of_spot(t), device_id_type=MESH,
-        )
+    y_all = many(ysend.at[pl.ds(0, PLANE - 1)], arecv.at[pl.ds(0, PLANE - 1)], ys, yr)
+    y_all.wait_recv()
 
     def translate(i, carry):
         y = yxc // 4
-        across = (1 - y // 2) * 2 + (y + i // 2) % 2
-        near = y // 2 * 2 + (y + 1 - (i // 2) % 2) % 2
-        pb = (box + 1 + i) % 2 * 4 + across + (near - across) * (i // 4)
+        pair = lax.div(i, 2)
+        across = (1 - y // 2) * 2 + lax.rem(y + pair, 2)
+        near = y // 2 * 2 + lax.rem(y + 3 - pair, 2)
+        row = jnp.where(pair < 2, across, near)
+        group = lax.rem(box + 1 + i, 2)
+        pb = group * 4 + row
         got = jnp.dot(oh[pb], arecv[...].reshape(512, 256), preferred_element_type=F32)
         real = imag = None
         for k in range(LINKED):
@@ -311,16 +293,15 @@
 
             @pl.when(s != slab)
             def _():
-                r_copy(s).start()
-
-        return carry
-
-    def r_wait(h, first):
-        def wait(i, carry):
-            r_arrival(h * 16 + (spot + i) % 16).wait_recv()
-            return carry
-
-        lax.fori_loop(first, 16, wait, 0)
+                pltpu.make_async_remote_copy(
+                    src_ref=rsend.at[s], dst_ref=rrecv.at[spot], send_sem=rs, recv_sem=rr.at[yxc // 8],
+                    device_id=(group, z * 16 + row * 4 + j), device_id_type=MESH,
+                ).start()
+
+        return carry
+
+    def r_wait(h, count):
+        many(rsend.at[pl.ds(0, count)], rrecv.at[pl.ds(0, count)], rs, rr.at[h]).wait_recv()
 
     def ungroup(h):
         for pair in range(2):
@@ -335,18 +316,18 @@
 
     def w_start(h):
         def start(i, carry):
-            z_copy(wsend, wrecv, ws, wr, h, order(i)).start()
+            z_copy(wsend, wrecv, ws, wr.at[h, z], h, order(i)).start()
             return carry
 
         lax.fori_loop(0, Z - 1, start, 0)
 
     lax.fori_loop(0, 6, translate, 0)
-    r_wait(half(0), 0)
+    r_wait(half(0), PLANE // 2)
     ungroup(half(0))
     w_start(half(0))
     lax.fori_loop(6, BLOCKS, translate, 0)
     rrecv[spot] = rsend[slab]
-    r_wait(half(1), 1)
+    r_wait(half(1), PLANE // 2 - 1)
     ungroup(half(1))
     w_start(half(1))
     for h in range(2):
@@ -356,12 +337,12 @@
     def descend(n, carry):
         terms = []
         for part in range(2):
-            i = n % (Z // 2) * 2 + part
-            h, zc = half(n // (Z // 2)), order(Z - 1 - i)
+            i = lax.rem(n, Z // 2) * 2 + part
+            h, zc = half(lax.div(n, Z // 2)), order(Z - 1 - i)
 
             @pl.when(i > 0)
             def _():
-                z_arrival(wsend, wrecv, ws, wr, h, zc).wait_recv()
+                many(wsend.at[h, zc], wrecv.at[h, zc], ws.at[h], wr.at[h, zc]).wait_recv()
 
             got = wrecv[h, zc].astype(F32)
             for parent in range(2):
@@ -378,21 +359,15 @@
         return carry
 
     lax.fori_loop(0, Z, descend, 0)
-    out_ref[...] = (acc[...] * 0.25).astype(BF16)
-
-    def z_sent(i, carry):
-        for h in range(2):
-            z_copy(zsend, zrecv, zs, zr, h, (z + i) % 8).wait_send()
-            z_copy(wsend, wrecv, ws, wr, h, (z + i) % 8).wait_send()
-        return carry
-
-    def plane_sent(i, carry):
-        y_copy((spot + i) % PLANE).wait_send()
-        r_copy((slab + i) % PLANE).wait_send()
-        return carry
-
-    lax.fori_loop(1, Z, z_sent, 0)
-    lax.fori_loop(1, PLANE, plane_sent, 0)
+    out_ref[...] = acc[...].astype(BF16)
+
+    for h in range(2):
+        z_all(h).wait_send()
+        most = (h, pl.ds(0, Z - 1))
+        many(wsend.at[most], wrecv.at[most], ws.at[h], wr.at[h, 0]).wait_send()
+    y_all.wait_send()
+    r_most = pl.ds(0, PLANE - 1)
+    many(rsend.at[r_most], rrecv.at[r_most], rs, rr.at[0]).wait_send()
 
 
 def local(leaf_patterns, octant, interp, shift_angle, partners, types, translators):
@@ -436,8 +411,8 @@
             pltpu.VMEM((2, Z, 32, HALF), BF16),
             pltpu.VMEM((2, rows, HALF), BF16),
             pltpu.VMEM((rows, low), F32),
-            dma((2 * Z,)), dma((2, Z)), dma((2, Z)), dma((PLANE,)), dma((PLANE,)), dma((2,)), dma((2,)),
-            dma((PLANE,)), dma((PLANE,)), dma((2, Z)), dma((2, Z)),
+            dma((2 * Z,)), dma((2,)), dma((2,)), dma, dma, dma((2,)), dma((2,)),
+            dma, dma((2,)), dma((2,)), dma((2, Z)),
         ],
         compiler_params=pltpu.CompilerParams(
             collective_id=0, has_side_effects=True, vmem_limit_bytes=58 * 1024 * 1024
@@ -451,7 +426,7 @@
         types.T,
         translators.transpose(1, 2, 0).reshape(-1, offsets),
     )
-    return out.reshape(boxes, pairs, excite, low)
+    return out.reshape(boxes, pairs, excite, low) * jnp.asarray(low / high, BF16)
 
 
 def solution(mesh):

time: 52.7 us -> 48.9 us (0.928)
  Pallas kernels: 50.7 us -> 46.8 us
  other arithmetic: 0 us -> 1.88 us
  local copies, waits for them, and re-layouts: 1.88 us -> 0 us
    pallas_call x1, Pallas kernels: 50.7 us -> 46.8 us  [local(): pl.pallas_call(kernel, out_shape=jax.ShapeDtypeStruct((rows, low), BF16),...]
    mul x0 -> x1, other arithmetic: none -> 1.88 us  [local(): out.reshape(boxes, pairs, excite, low) * jnp.asarray(low / high, BF16)]
    unnamed x1 -> x0, local copies, waits for them, and re-layouts: 1.88 us -> none
where the time goes in v4:
time: 48.9 us; the launch traced here: 48.7 us
  Pallas kernels  46.8 us (96%)
  other arithmetic  1.88 us (4%)
    pallas_call x1, Pallas kernels, local(): pl.pallas_call(kernel, out_shape=jax.ShapeDtypeStruct((rows, low), BF16),...  46.8 us
    mul x1, other arithmetic, local(): out.reshape(boxes, pairs, excite, low) * jnp.asarray(low / high, BF16)  1.88 us

profile of v4, /device:TPU:1, one launch (start us, length us, event | category | flops | bytes accessed | tf_op | source)
XLA Modules:
  0.0 48.7 jit_solution(15467005420428682516)
XLA Ops:
  0.0 46.8 %shard_map.73 = bf16[256,1024]{1,0:T(8,128)(2,1)} custom-call(s32[16]{0:T(128)} %oct_ref.1, bf16[256,1024]{1,0:T(8,128)(2,1)} %bitcast.7, bf16[1024,4096]{1,0:T(8,128)(2,1)} %interp_ref.1, f32[8,4096]{1,0:T(8,128)} %angle_hbm.1, s32[27,256]{1,0:T(8,128)} %bitcast.9, s32[27,256]{1,0:T(8,128)} %bitcast.10, f32[64,343]{1,0:T(8,128)} %bitcast.8), custom_call_target="tpu_custom_call" | custom-call | tf_op jit(solution)/shard_map/pallas_call | solution.py:381
  46.8 1.9 %broadcast_multiply_fusion = bf16[256,1024]{1,0:T(8,128)(2,1)} fusion(bf16[256,1024]{1,0:T(8,128)(2,1)} %shard_map.73), kind=kLoop, calls=%fused_computation | loop fusion | flops 262144 | bytes 1048576 | tf_op jit(solution)/shard_map/mul | solution.py:429

commit v5 on v4

--- a/solution.py
+++ b/solution.py
@@ -99,9 +99,9 @@
             greet((group, z * 16 + wrap(yxc + i, 16)))
         return carry
 
-    lax.fori_loop(1, Z, greet_z, 0)
+    lax.fori_loop(1, Z, greet_z, 0, unroll=True)
     greet((1 - box, d))
-    lax.fori_loop(1, 16, greet_plane, 0)
+    lax.fori_loop(1, 16, greet_plane, 0, unroll=True)
 
     def many(src, dst, ssem, rsem):
         return pltpu.make_async_remote_copy(
@@ -247,17 +247,17 @@
 
         return start
 
-    lax.fori_loop(0, 1, factors, 0)
+    lax.fori_loop(0, 2, factors, 0)
     z_all(half(0)).wait_recv()
     regroup(half(0))
-    lax.fori_loop(0, 8, y_starts(half(0)), 0)
-    lax.fori_loop(1, 5, factors, 0)
+    lax.fori_loop(0, 8, y_starts(half(0)), 0, unroll=True)
+    lax.fori_loop(2, 6, factors, 0)
     z_all(half(1)).wait_recv()
     regroup(half(1))
     y_start(1 - box, yxc)
-    lax.fori_loop(1, 8, y_starts(half(1)), 0)
+    lax.fori_loop(1, 8, y_starts(half(1)), 0, unroll=True)
     arecv[slab] = ysend[spot]
-    lax.fori_loop(5, BLOCKS, factors, 0)
+    lax.fori_loop(6, BLOCKS, factors, 0)
 
     def sources(pb, carry):
         index = indices(pb)
@@ -319,13 +319,13 @@
             z_copy(wsend, wrecv, ws, wr.at[h, z], h, order(i)).start()
             return carry
 
-        lax.fori_loop(0, Z - 1, start, 0)
-
-    lax.fori_loop(0, 6, translate, 0)
+        lax.fori_loop(0, Z - 1, start, 0, unroll=True)
+
+    lax.fori_loop(0, 7, translate, 0)
     r_wait(half(0), PLANE // 2)
     ungroup(half(0))
     w_start(half(0))
-    lax.fori_loop(6, BLOCKS, translate, 0)
+    lax.fori_loop(7, BLOCKS, translate, 0)
     rrecv[spot] = rsend[slab]
     r_wait(half(1), PLANE // 2 - 1)
     ungroup(half(1))

time: 48.9 us -> 47.9 us (0.980)
  Pallas kernels: 46.8 us -> 45.9 us
    pallas_call x1, Pallas kernels: 46.8 us -> 45.9 us  [local(): pl.pallas_call(kernel, out_shape=jax.ShapeDtypeStruct((rows, low), BF16),...]
where the time goes in v5:
time: 47.9 us; the launch traced here: 47.8 us
  Pallas kernels  45.9 us (96%)
  other arithmetic  1.88 us (4%)
    pallas_call x1, Pallas kernels, local(): pl.pallas_call(kernel, out_shape=jax.ShapeDtypeStruct((rows, low), BF16),...  45.9 us
    mul x1, other arithmetic, local(): out.reshape(boxes, pairs, excite, low) * jnp.asarray(low / high, BF16)  1.88 us

profile of v5, /device:TPU:1, one launch (start us, length us, event | category | flops | bytes accessed | tf_op | source)
XLA Modules:
  0.0 47.8 jit_solution(14781957657719134461)
XLA Ops:
  0.0 45.9 %shard_map.73 = bf16[256,1024]{1,0:T(8,128)(2,1)} custom-call(s32[16]{0:T(128)} %oct_ref.1, bf16[256,1024]{1,0:T(8,128)(2,1)} %bitcast.7, bf16[1024,4096]{1,0:T(8,128)(2,1)} %interp_ref.1, f32[8,4096]{1,0:T(8,128)} %angle_hbm.1, s32[27,256]{1,0:T(8,128)} %bitcast.9, s32[27,256]{1,0:T(8,128)} %bitcast.10, f32[64,343]{1,0:T(8,128)} %bitcast.8), custom_call_target="tpu_custom_call" | custom-call | tf_op jit(solution)/shard_map/pallas_call | solution.py:381
  45.9 1.9 %broadcast_multiply_fusion = bf16[256,1024]{1,0:T(8,128)(2,1)} fusion(bf16[256,1024]{1,0:T(8,128)(2,1)} %shard_map.73), kind=kLoop, calls=%fused_computation | loop fusion | flops 262144 | bytes 1048576 | tf_op jit(solution)/shard_map/mul | solution.py:429
